TPU v7x, 256 devices: a whole 4x4x8 slice. The times are simulated.
256 devices in a mesh: row: 4 (over y_lo, core), col: 64 (over x, y_hi, z).
Axes of the slice: x: 4, y: 4 (y_hi: 2, y_lo: 2; y = y_hi * 2 + y_lo), z: 8, core: 2. Of those that a mesh axis runs over, the one named last changes fastest.
Arguments:
- tensor: bfloat16 [128, 3072, 4096], P(None, 'col', 'row'), may hold values from -6 to 6
- first_factor: bfloat16 [64, 4096], P(None, ('row', 'col')), may hold values from -0.453125 to 0.453125
- second_factor: bfloat16 [64, 3072], P(None, 'col'), may hold values from -0.5232237 to 0.5232237
Outputs:
- frames: float32 [64, 128], replicated
- mode_one: float32 [64, 4096], P(None, ('row', 'col'))
All inputs are finite; a program needn't handle non-finite values.
Results may differ from a plain program's by a relative error of at most 0.004.
Values may be sent and summed in bfloat16 or wider, within the bound.
A program may use at most 128 MiB of HBM per device.

v0:
```python
import jax
import jax.numpy as jnp
from jax import lax
from jax.sharding import PartitionSpec as P

ridge_weight = 0.05


def ridge_solve(gram, right_side):
    order_size = gram.shape[0]
    factor_low = jnp.linalg.cholesky(gram + ridge_weight * jnp.eye(order_size, dtype=jnp.float32))
    middle = lax.linalg.triangular_solve(factor_low, right_side, left_side=True, lower=True)
    return lax.linalg.triangular_solve(
        factor_low, middle, left_side=True, lower=True, transpose_a=True
    )


def gram_of(factor):
    return jnp.dot(factor, factor.T, preferred_element_type=jnp.float32)


def spread_product(frames, second):
    product = frames[:, :, None] * second[:, None, :]
    return product.astype(jnp.bfloat16).reshape(frames.shape[0], -1)


def project_columns(flattened, portion):
    return lax.dot_general(
        portion, flattened, (((1,), (1,)), ((), ())), preferred_element_type=jnp.float32
    )


def local(tensor, first_factor, second_factor):
    frame_count, col_count, row_count = tensor.shape
    components = first_factor.shape[0]
    flattened = tensor.reshape(frame_count * col_count, row_count)
    second_values = second_factor.astype(jnp.float32)
    share_rows = row_count // lax.axis_size("col")
    gram_first = lax.psum(gram_of(first_factor), ("row", "col"))
    gram_second = lax.psum(gram_of(second_factor), "col")
    projected = project_columns(flattened, lax.all_gather(first_factor, "col", axis=1, tiled=True))
    projected = projected.reshape(components, frame_count, col_count)
    frame_part = jnp.einsum("rkj,rj->rk", projected, second_values, precision=lax.Precision.HIGHEST)
    frame_sum = lax.psum(frame_part, ("row", "col"))
    frames = ridge_solve(gram_first * gram_second, frame_sum)
    gram_frames = jnp.dot(frames, frames.T, precision=lax.Precision.HIGHEST)
    weights = spread_product(frames, second_values)
    full_part = lax.dot_general(
        weights, flattened, (((1,), (0,)), ((), ())), preferred_element_type=jnp.float32
    )
    first_sum = lax.psum(full_part, "col")
    new_first = ridge_solve(gram_second * gram_frames, first_sum).astype(jnp.bfloat16)
    gram_new = lax.psum(gram_of(new_first), "row")
    projected_new = lax.dot_general(
        new_first, flattened, (((1,), (1,)), ((), ())), preferred_element_type=jnp.float32
    )
    projected_new = projected_new.reshape(components, frame_count, col_count)
    second_part = jnp.einsum("rkj,rk->rj", projected_new, frames, precision=lax.Precision.HIGHEST)
    second_sum = lax.psum(second_part, "row")
    new_second = ridge_solve(gram_new * gram_frames, second_sum)
    weights_next = spread_product(frames, new_second)
    full_next = lax.dot_general(
        weights_next, flattened, (((1,), (0,)), ((), ())), preferred_element_type=jnp.float32
    )
    summed = lax.psum(full_next, "col")
    mode_one = lax.dynamic_slice_in_dim(summed, lax.axis_index("col") * share_rows, share_rows, 1)
    return (frames, mode_one)


def solution(mesh):
    return jax.shard_map(
        local,
        mesh=mesh,
        in_specs=(P(None, "col", "row"), P(None, ("row", "col")), P(None, "col")),
        out_specs=(P(), P(None, ("row", "col"))),
        check_vma=False,
    )
```

profile of v0, /device:TPU:24, one launch (start us, length us, event | category | flops | bytes accessed | tf_op | source)
XLA Modules:
  0.0 2019.9 jit_solution(1604844099440439791)
XLA Ops:
  7.2 164.3 %all_gather.3 = bf16[64,1024]{0,1:T(8,128)(2,1)S(1)} all-gather(bf16[64,16]{0,1:T(8,128)(2,1)} %param.5), channel_id=1, replica_groups=mesh['row'=4,'col'=64] {'col'}, dimensions={1}, use_global_device_ids=true | all-gather | bytes 133120 | tf_op jit(solution)/shard_map/all_gather | solution.py:41
  171.5 0.9 fusion.29
  172.4 1.0 fusion.30
  173.4 0.7 convert_element_type.15
  174.1 17.8 copy.28
  192.0 350.9 %psum.50 = f32[64,64]{1,0:T(8,128)S(1)} all-reduce(f32[64,64]{1,0:T(8,128)S(1)} %fusion.30), channel_id=1, replica_groups=mesh['row'=4,'col'=64] {'col'}, use_global_device_ids=true, to_apply=%region_1.0 | all-reduce | flops 4096 | bytes 32768 | tf_op jit(solution)/shard_map/psum | solution.py:40
  542.9 6.9 fusion.8
  549.8 1.7 fusion.2
  551.5 93.3 %all-reduce = (f32[64,128]{1,0:T(8,128)S(1)}, f32[64,64]{1,0:T(8,128)S(1)}) all-reduce(f32[64,128]{1,0:T(8,128)S(1)} %bitcast.73, f32[64,64]{1,0:T(8,128)S(1)} %fusion.29), channel_id=1, replica_groups=mesh['row'=4,'col'=64] {'row','col'}, use_global_device_ids=true, to_apply=%region_4.0 | all-reduce | flops 12288 | bytes 98304 | tf_op jit(solution)/shard_map/psum | solution.py:44
  645.0 5.9 cholesky.59
  652.2 4.9 custom-call.17
  657.5 7.6 convolution_bitcast_fusion.1
  665.7 5.9 cholesky.70
  672.9 4.9 custom-call.18
  677.8 610.1 %all-reduce.5.cloned.1.call-done = f32[64,1024]{1,0:T(8,128)} async-done(((f32[64,1024]{1,0:T(8,128)}), f32[64,1024]{1,0:T(8,128)}) %all-reduce.5.cloned.1.call-update) | async-done | bytes 262160 | tf_op jit(solution)/shard_map/psum | solution.py:51
  1287.9 1.4 fusion.21
  1289.6 6.9 fusion.10
  1296.6 3.3 fusion
  1300.0 10.7 all-reduce.1
  1310.9 5.9 cholesky.81
  1318.1 4.9 custom-call.19
  1323.4 7.3 convolution_bitcast_fusion
  1330.8 681.0 %all-reduce.7.cloned.1.call-done = f32[64,1024]{0,1:T(8,128)} async-done(((f32[64,1024]{0,1:T(8,128)}), f32[64,1024]{0,1:T(8,128)}) %all-reduce.7.cloned.1.call-update) | async-done | bytes 262160 | tf_op jit(solution)/shard_map/psum | solution.py:65
  2011.8 1.3 constant_dynamic-slice_fusion
  (36 shorter events, 6.4 us)
Async XLA Ops:
  7.2 1280.7 %all-reduce.5.cloned.1.call-start = ((), (), s32[]{:S(2)}) async-start(), calls=%async_computation | async-start | bytes 524288 | tf_op jit(solution)/shard_map/psum | solution.py:51
  174.1 17.8 copy-start.1
  657.5 665.9 %copy-start = (f32[64,128]{1,0:T(8,128)}, f32[64,128]{1,0:T(8,128)S(1)}, u32[]{:S(2)}) copy-start(f32[64,128]{1,0:T(8,128)S(1)} %fusion.24) | copy-start | bytes 98308
  665.1 1346.6 %all-reduce.7.cloned.1.call-start = ((), (), s32[]{:S(2)}) async-start(), calls=%async_computation.1 | async-start | bytes 1048576 | tf_op jit(solution)/shard_map/psum | solution.py:65
Sparse Core Ops, SparseCore 0:
  665.2 622.5 all-reduce.4
  1330.9 680.8 all-reduce.6
where the time goes:
time: 2030 us; the launch traced here: 2020 us
  waiting for transfers between devices  1290 us (64%)
  blocking collectives  619 us (30%)
  matrix products  38.5 us (2%)
  other arithmetic  37 us (2%)
    psum x1, waiting for transfers between devices, local(): summed = lax.psum(full_next, 'col')  681 us
    psum x1, waiting for transfers between devices, local(): first_sum = lax.psum(full_part, 'col')  610 us
    psum x1, blocking collectives, local(): gram_second = lax.psum(gram_of(second_factor), 'col')  351 us
    all_gather x1, blocking collectives, local(): lax.all_gather(first_factor, 'col', axis=1, tiled=True)  164 us
    psum x1, blocking collectives, local(): frame_sum = lax.psum(frame_part, ('row', 'col'))  93.3 us
  transfers between devices with their start and end apart: 2, of which 2 were waited for; matrix products, arithmetic and copies ran while one was open for 1% of the time, Pallas kernels for 0%

commit v1 on v0

v1 whole, which is shorter than its diff:
```python
import functools

import jax
import jax.numpy as jnp
from jax import lax
from jax.experimental import pallas as pl
from jax.experimental.pallas import tpu as pltpu
from jax.sharding import PartitionSpec as P

ridge_weight = 0.05
MESH_ID = pl.DeviceIdType.MESH


def ridge_solve(gram, right_side):
    order_size = gram.shape[0]
    factor_low = jnp.linalg.cholesky(gram + ridge_weight * jnp.eye(order_size, dtype=jnp.float32))
    middle = lax.linalg.triangular_solve(factor_low, right_side, left_side=True, lower=True)
    return lax.linalg.triangular_solve(
        factor_low, middle, left_side=True, lower=True, transpose_a=True
    )


def gram_of(factor):
    return jnp.dot(factor, factor.T, preferred_element_type=jnp.float32)


def spread_product(frames, second):
    product = frames[:, :, None] * second[:, None, :]
    return product.astype(jnp.bfloat16).reshape(frames.shape[0], -1)


def _exchange_kernel(n, broadcast, reduce, send_ref, out_ref, recv, send_sems, recv_sems):
    me = lax.axis_index("col")
    row = lax.axis_index("row")

    def source(peer):
        return send_ref if broadcast else send_ref.at[peer]

    def descriptor(peer, slot):
        return pltpu.make_async_remote_copy(
            src_ref=source(peer),
            dst_ref=recv.at[slot],
            send_sem=send_sems.at[peer],
            recv_sem=recv_sems.at[slot],
            device_id=(row, peer),
            device_id_type=MESH_ID,
        )

    barrier = pltpu.get_barrier_semaphore()

    def greet(t, carry):
        peer = lax.rem(me + 1 + t, n)
        pl.semaphore_signal(barrier, inc=1, device_id=(row, peer), device_id_type=MESH_ID)
        return carry

    lax.fori_loop(0, n - 1, greet, 0)
    pl.semaphore_wait(barrier, n - 1)

    def start(t, carry):
        peer = lax.rem(me + 1 + t, n)
        descriptor(peer, me).start()
        return carry

    lax.fori_loop(0, n - 1, start, 0)

    def finish(t, carry):
        peer = lax.rem(me + 1 + t, n)
        copy = descriptor(peer, peer)
        copy.wait_send()
        copy.wait_recv()
        return carry

    lax.fori_loop(0, n - 1, finish, 0)
    recv[me] = source(me)[...]
    if reduce:
        out_ref[...] = jnp.sum(recv[...], axis=0)
    else:
        out_ref[...] = recv[...]


def col_exchange(send, n, broadcast, reduce, collective_id):
    piece = send.shape if broadcast else send.shape[1:]
    out_shape = piece if reduce else (n,) + tuple(piece)
    return pl.pallas_call(
        functools.partial(_exchange_kernel, n, broadcast, reduce),
        out_shape=jax.ShapeDtypeStruct(tuple(out_shape), send.dtype),
        in_specs=[pl.BlockSpec(memory_space=pltpu.VMEM)],
        out_specs=pl.BlockSpec(memory_space=pltpu.VMEM),
        scratch_shapes=[
            pltpu.VMEM((n,) + tuple(piece), send.dtype),
            pltpu.SemaphoreType.DMA((n,)),
            pltpu.SemaphoreType.DMA((n,)),
        ],
        compiler_params=pltpu.CompilerParams(collective_id=collective_id, has_side_effects=True),
    )(send)


def col_gather_t(piece, n):
    gathered = col_exchange(piece, n, broadcast=True, reduce=False, collective_id=0)
    return gathered.reshape(n * piece.shape[0], piece.shape[1])


def col_reduce_scatter_t(full_t, n, collective_id):
    width = full_t.shape[0] // n
    return col_exchange(
        full_t.reshape(n, width, full_t.shape[1]), n, broadcast=False, reduce=True,
        collective_id=collective_id,
    )


def local(tensor, first_factor, second_factor):
    frame_count, col_count, row_count = tensor.shape
    components = first_factor.shape[0]
    n = lax.axis_size("col")
    flattened = tensor.reshape(frame_count * col_count, row_count)
    second_values = second_factor.astype(jnp.float32)
    gram_first_part = gram_of(first_factor)
    gram_second_part = gram_of(second_factor) * (1.0 / lax.axis_size("row"))
    block_t = col_gather_t(first_factor.T, n)
    projected = lax.dot_general(
        block_t, flattened, (((0,), (1,)), ((), ())), preferred_element_type=jnp.float32
    )
    projected = projected.reshape(components, frame_count, col_count)
    frame_part = jnp.einsum("rkj,rj->rk", projected, second_values, precision=lax.Precision.HIGHEST)
    frame_sum, gram_first, gram_second = lax.psum(
        (frame_part, gram_first_part, gram_second_part), ("row", "col")
    )
    frames = ridge_solve(gram_first * gram_second, frame_sum)
    gram_frames = jnp.dot(frames, frames.T, precision=lax.Precision.HIGHEST)
    weights = spread_product(frames, second_values)
    full_part_t = lax.dot_general(
        flattened, weights, (((0,), (1,)), ((), ())), preferred_element_type=jnp.float32
    )
    first_sum_mine = col_reduce_scatter_t(full_part_t, n, 1).T
    new_first_mine = ridge_solve(gram_second * gram_frames, first_sum_mine).astype(jnp.bfloat16)
    new_block_t = col_gather_t(new_first_mine.T, n)
    gram_new_part = lax.dot_general(
        new_block_t, new_block_t, (((0,), (0,)), ((), ())), preferred_element_type=jnp.float32
    )
    projected_new = lax.dot_general(
        new_block_t, flattened, (((0,), (1,)), ((), ())), preferred_element_type=jnp.float32
    )
    projected_new = projected_new.reshape(components, frame_count, col_count)
    second_part = jnp.einsum("rkj,rk->rj", projected_new, frames, precision=lax.Precision.HIGHEST)
    second_sum, gram_new = lax.psum((second_part, gram_new_part), "row")
    new_second = ridge_solve(gram_new * gram_frames, second_sum)
    weights_next = spread_product(frames, new_second)
    full_next_t = lax.dot_general(
        flattened, weights_next, (((0,), (1,)), ((), ())), preferred_element_type=jnp.float32
    )
    mode_one = col_reduce_scatter_t(full_next_t, n, 2).T
    return (frames, mode_one)


def solution(mesh):
    return jax.shard_map(
        local,
        mesh=mesh,
        in_specs=(P(None, "col", "row"), P(None, ("row", "col")), P(None, "col")),
        out_specs=(P(), P(None, ("row", "col"))),
        check_vma=False,
    )
```

time: 2030 us -> 527 us (0.26)
  waiting for transfers between devices: 1290 us -> 241 us
  blocking collectives: 619 us -> 11 us
  Pallas kernels: 0 us -> 90.6 us
  matrix products: 38.5 us -> 118 us
    psum x2 -> x1, waiting for transfers between devices: 1290 us -> 241 us  [local(): lax.psum((frame_part, gram_first_part, gram_second_part), ('row', 'col'))]
    psum x3 -> x1, blocking collectives: 455 us -> 11 us  [local(): second_sum, gram_new = lax.psum((second_part, gram_new_part), 'row')]
    all_gather x1 -> x0, blocking collectives: 164 us -> none  [local(): lax.all_gather(first_factor, 'col', axis=1, tiled=True)]
    pallas_call x0 -> x4, Pallas kernels: none -> 90.6 us  [col_exchange(): pl.pallas_call(functools.partial(_exchange_kernel, n, broadcast, reduce),...]
    dot_general x4 -> x5, matrix products: 28.7 us -> 105 us  [the longest x1 34.3 us: local(): lax.dot_general(new_block_t, flattened, (((0,), (1,)), ((), ())), preferr...]
  transfers between devices with their start and end apart: 2 -> 1, of which waited for: 2 -> 1; matrix products, arithmetic and copies ran while one was open for 1% -> 0% of each run, Pallas kernels for 0% -> 0%
where the time goes in v1:
time: 527 us; the launch traced here: 517 us
  waiting for transfers between devices  241 us (46%)
  matrix products  118 us (22%)
  Pallas kernels  90.6 us (17%)
  other arithmetic  37.1 us (7%)
  between operations  14.7 us (3%)
  blocking collectives  11 us (2%)
    psum x1, waiting for transfers between devices, local(): lax.psum((frame_part, gram_first_part, gram_second_part), ('row', 'col'))  241 us
    pallas_call x4, Pallas kernels, col_exchange(): pl.pallas_call(functools.partial(_exchange_kernel, n, broadcast, reduce),...  90.6 us
    dot_general x1, matrix products, local(): lax.dot_general(new_block_t, flattened, (((0,), (1,)), ((), ())), preferr...  34.3 us
    dot_general x1, matrix products, local(): lax.dot_general(block_t, flattened, (((0,), (1,)), ((), ())), preferred_e...  23.5 us
    dot_general x1, matrix products, local(): lax.dot_general(flattened, weights_next, (((0,), (1,)), ((), ())), prefer...  23.3 us
    dot_general x1, matrix products, local(): lax.dot_general(flattened, weights, (((0,), (1,)), ((), ())), preferred_e...  23 us
    another operation x9, other arithmetic, ridge_solve(): jnp.linalg.cholesky(gram + ridge_weight * jnp.eye(order_size, dtype=jnp.f...  19.6 us
    another operation x6, other arithmetic, ridge_solve(): lax.linalg.triangular_solve(factor_low, middle, left_side=True, lower=Tru...  16.6 us
  transfers between devices with their start and end apart: 1, of which 1 were waited for; matrix products, arithmetic and copies ran while one was open for 0% of the time, Pallas kernels for 0%

profile of v1, /device:TPU:24, one launch (start us, length us, event | category | flops | bytes accessed | tf_op | source)
XLA Modules:
  0.0 517.3 jit_solution(12548862814570012237)
XLA Ops:
  7.2 1.5 fusion.40
  8.7 22.5 %shard_map.50 = bf16[64,16,64]{2,1,0:T(8,128)(2,1)} custom-call(bf16[16,64]{1,0:T(8,128)(2,1)} %bitcast.85), custom_call_target="tpu_custom_call" | custom-call | tf_op jit(solution)/shard_map/pallas_call | solution.py:84
  31.3 1.6 convolution_multiply_fusion
  33.7 23.5 %fusion.6 = f32[64,128,48]{1,0,2:T(8,128)S(1)} fusion(bf16[1024,64,1]{1,0,2:T(8,128)(2,1)} %bitcast.80, bf16[128,48,1024]{2,1,0:T(8,128)(2,1)} %param.4), kind=kOutput, calls=%fused_computation.6 | convolution fusion | flops 805306368 | bytes 14286848 | tf_op jit(solution)/shard_map/dot_general | solution.py:120
  57.1 2.3 fusion.10
  59.5 241.2 %all-reduce.4.cloned.1.call-done = (f32[64,128]{1,0:T(8,128)}, f32[64,64]{1,0:T(8,128)}, f32[64,64]{1,0:T(8,128)}) async-done(((f32[64,128]{1,0:T(8,128)}, f32[64,64]{1,0:T(8,128)}, f32[64,64]{1,0:T(8,128)}), (f32[64,128]{1,0:T(8,128)}, f32[64,64]{1,0:T(8,128)}, f32[64,64]{1,0:T(8,128)})) %all-reduce.4.cloned.1.call-update) | async-done | bytes 65552 | tf_op jit(solution)/shard_map/psum | solution.py:125
  301.6 5.9 %cholesky.59 = f32[64,64]{1,0:T(8,128)S(1)} custom-call(f32[64,64]{1,0:T(8,128)S(1)} %copy.30), custom_call_target="Cholesky" | custom-call | tf_op jit(solution)/shard_map/jit(cholesky)/cholesky | solution.py:16
  308.8 4.9 custom-call.17
  313.7 1.0 fusion.37
  316.1 5.9 %cholesky.70 = f32[64,64]{1,0:T(8,128)S(1)} custom-call(f32[64,64]{1,0:T(8,128)S(1)} %copy.34), custom_call_target="Cholesky" | custom-call | tf_op jit(solution)/shard_map/jit(cholesky)/cholesky | solution.py:16
  323.3 4.9 custom-call.18
  328.2 23.0 %fusion.12 = f32[1024,64]{0,1:T(8,128)S(1)} fusion(bf16[128,48,1024]{2,1,0:T(8,128)(2,1)} %param.4, f32[64,48]{0,1:T(8,128)S(1)} %convert_element_type.16, f32[64,128]{1,0:T(8,128)S(1)} %fusion.35), kind=kOutput, calls=%fused_computation.14 | convolution fusion | flops 806092800 | bytes 12890112 | tf_op jit(solution)/shard_map/dot_general | solution.py:131
  351.2 1.0 copy.36
  352.2 25.0 %shard_map.51 = f32[16,64]{1,0:T(8,128)} custom-call(f32[64,16,64]{2,1,0:T(8,128)} %bitcast.77), custom_call_target="tpu_custom_call" | custom-call | tf_op jit(solution)/shard_map/pallas_call | solution.py:84
  378.9 18.5 %shard_map.52 = bf16[64,16,64]{2,1,0:T(8,128)(2,1)} custom-call(bf16[16,64]{1,0:T(8,128)(2,1)} %convolution_convert_fusion.send_ref), custom_call_target="tpu_custom_call" | custom-call | tf_op jit(solution)/shard_map/pallas_call | solution.py:84
  397.3 1.3 convolution_bitcast_fusion
  398.6 34.3 %fusion.2 = f32[64,128,48]{1,0,2:T(8,128)S(1)} fusion(bf16[1024,64,1]{1,0,2:T(8,128)(2,1)} %bitcast.81, bf16[128,48,1024]{2,1,0:T(8,128)(2,1)} %param.4), kind=kOutput, calls=%fused_computation.2 | convolution fusion | flops 805306368 | bytes 14286848 | tf_op jit(solution)/shard_map/dot_general | solution.py:140
  432.9 3.3 fusion.8
  436.2 11.0 %all-reduce.1 = (f32[64,48]{1,0:T(8,128)S(1)}, f32[64,64]{1,0:T(8,128)S(1)}) all-reduce(f32[64,48]{1,0:T(8,128)S(1)} %bitcast.84, f32[64,64]{1,0:T(8,128)S(1)} %convolution_bitcast_fusion), channel_id=1, replica_groups=mesh['row'=4,'col'=64] {'row'}, use_global_device_ids=true, to_apply=%region_6.8 | all-reduce | flops 7168 | bytes 57344 | tf_op jit(solution)/shard_map/psum | solution.py:145
  447.4 5.9 %cholesky.81 = f32[64,64]{1,0:T(8,128)S(1)} custom-call(f32[64,64]{1,0:T(8,128)S(1)} %copy.40), custom_call_target="Cholesky" | custom-call | tf_op jit(solution)/shard_map/jit(cholesky)/cholesky | solution.py:16
  454.6 4.9 custom-call.19
  460.0 23.3 %fusion.15 = f32[1024,64]{0,1:T(8,128)S(1)} fusion(bf16[128,48,1024]{2,1,0:T(8,128)(2,1)} %param.4, f32[64,48]{0,1:T(8,128)S(1)} %fusion.26, f32[64,128]{1,0:T(8,128)S(1)} %fusion.35), kind=kOutput, calls=%fused_computation.15 | convolution fusion | flops 806092800 | bytes 12890112 | tf_op jit(solution)/shard_map/dot_general | solution.py:148
  484.2 24.6 %shard_map.53 = f32[16,64]{1,0:T(8,128)} custom-call(f32[64,16,64]{2,1,0:T(8,128)} %bitcast.78), custom_call_target="tpu_custom_call" | custom-call | tf_op jit(solution)/shard_map/pallas_call | solution.py:84
  508.8 1.3 copy.77
  (35 shorter events, 10.3 us)
Async XLA Ops:
  7.2 293.5 %all-reduce.4.cloned.1.call-start = ((), (), s32[]{:S(2)}) async-start(), calls=%async_computation | async-start | bytes 196608 | tf_op jit(solution)/shard_map/psum | solution.py:125
  57.1 2.4 copy-start.1
  314.9 145.0 %copy-start = (f32[64,128]{1,0:T(8,128)}, f32[64,128]{1,0:T(8,128)S(1)}, u32[]{:S(2)}) copy-start(f32[64,128]{1,0:T(8,128)S(1)} %fusion.35) | copy-start | bytes 98308
Sparse Core Ops, SparseCore 0:
  59.6 241.0 all-reduce.3
